TPU v7x, 256 devices: a whole 4x4x8 slice. The times are simulated.
256 devices in a mesh: pipe: 4 (over x), seq: 64 (over y, z, core).
Axes of the slice: x: 4, y: 4, z: 8, core: 2. Of those that a mesh axis runs over, the one named last changes fastest.
Arguments:
- acts: bfloat16 [4, 16384, 1024], P('pipe', 'seq'), may hold values from -6 to 6
- cotan: bfloat16 [4, 16384, 1024], P('pipe', 'seq'), may hold values from -6 to 6
- proj_in: bfloat16 [4, 1024, 2048], P('pipe'), may hold values from -0.1875 to 0.1875
- proj_out: bfloat16 [4, 1024, 1024], P('pipe'), may hold values from -0.1875 to 0.1875
- block_mix: bfloat16 [4, 16384, 256], P('pipe', 'seq'), may hold values from -0.375 to 0.375
- twiddle: float32 [4, 6, 2, 2, 1024], P('pipe'), may hold values from -2.5 to 2.5
Outputs:
- mixed: bfloat16 [4, 16384, 1024], P('pipe', 'seq')
- grad_prev: bfloat16 [4, 16384, 1024], P('pipe', 'seq')
- grad_in_proj: float32 [4, 1024, 2048], P('pipe', 'seq')
- grad_out_proj: float32 [4, 1024, 1024], P('pipe', 'seq')
- grad_block_mix: float32 [4, 16384, 256], P('pipe', 'seq')
- grad_twiddle: float32 [4, 6, 2, 2, 1024], P('pipe')
All inputs are finite; a program needn't handle non-finite values.
Results may differ from a plain program's by a relative error of at most 0.014.
Values may be sent and summed in bfloat16 or wider, within the bound.
A program may use at most 128 MiB of HBM per device.

v0:
```python
import jax
import jax.numpy as jnp
from jax import lax
from jax.sharding import PartitionSpec as P


def swapped(block, axis, apart):
    count = lax.axis_size(axis)
    route = []
    for low in range(count):
        high = low | 1 << apart
        if high != low and high < count:
            route += [(low, high), (high, low)]
    return lax.ppermute(block, axis, route)


def from_behind(value, axis, steps):
    count = lax.axis_size(axis)
    first, last = (max(0, -steps), min(count, count - steps))
    return lax.ppermute(value, axis, [(source, source + steps) for source in range(first, last)])


def on_device(acts, cotan, proj_in, proj_out, block_mix, twiddle):
    inputs = acts[0]
    grad_out = cotan[0]
    w_in = proj_in[0]
    w_out = proj_out[0]
    square_mix = block_mix[0]
    twiddle_w = twiddle[0]
    row_count, feature_count = inputs.shape
    seq_count = lax.axis_size("seq")
    segment_total = seq_count.bit_length() - 1
    position = lax.axis_index("seq")
    projected = jnp.dot(inputs, w_in, preferred_element_type=jnp.float32)
    value = projected[:, :feature_count].astype(jnp.bfloat16)
    gate = projected[:, feature_count:].astype(jnp.bfloat16)
    first_segment = jnp.dot(square_mix, value, preferred_element_type=jnp.float32).astype(
        jnp.bfloat16
    )
    partials = [None] * segment_total
    stored = []
    current = first_segment
    for segment_bit in range(segment_total):
        partner = swapped(current, "seq", segment_bit)
        upper_half = position >> segment_bit & 1
        segment_coef = jnp.where(
            upper_half == 0, twiddle_w[segment_bit, 0], twiddle_w[segment_bit, 1]
        )
        stored.append((current, partner))
        current = (
            segment_coef[0] * current.astype(jnp.float32)
            + segment_coef[1] * partner.astype(jnp.float32)
        ).astype(jnp.bfloat16)
    hidden = (current.astype(jnp.float32) * gate.astype(jnp.float32)).astype(jnp.bfloat16)
    mixed_out = jnp.dot(hidden, w_out, preferred_element_type=jnp.float32).astype(jnp.bfloat16)
    d_hidden = lax.dot_general(
        grad_out, w_out, (((1,), (1,)), ((), ())), preferred_element_type=jnp.float32
    ).astype(jnp.bfloat16)
    wout_term = lax.dot_general(
        hidden, grad_out, (((0,), (0,)), ((), ())), preferred_element_type=jnp.float32
    )
    d_monarch = (d_hidden.astype(jnp.float32) * gate.astype(jnp.float32)).astype(jnp.bfloat16)
    d_gate = (d_hidden.astype(jnp.float32) * current.astype(jnp.float32)).astype(jnp.bfloat16)
    grad_now = d_monarch
    for segment_bit in range(segment_total - 1, -1, -1):
        grad_partner = swapped(grad_now, "seq", segment_bit)
        upper_half = position >> segment_bit & 1
        own_coef = jnp.where(upper_half == 0, twiddle_w[segment_bit, 0], twiddle_w[segment_bit, 1])
        peer_coef = jnp.where(upper_half == 0, twiddle_w[segment_bit, 1], twiddle_w[segment_bit, 0])
        saved_own, saved_peer = stored[segment_bit]
        grad_float = grad_now.astype(jnp.float32)
        own_row = jnp.stack(
            [
                jnp.sum(grad_float * saved_own.astype(jnp.float32), axis=0),
                jnp.sum(grad_float * saved_peer.astype(jnp.float32), axis=0),
            ]
        )
        empty_row = jnp.zeros_like(own_row)
        partials[segment_bit] = jnp.where(
            upper_half == 0, jnp.stack([own_row, empty_row]), jnp.stack([empty_row, own_row])
        )
        grad_now = (
            own_coef[0] * grad_float + peer_coef[1] * grad_partner.astype(jnp.float32)
        ).astype(jnp.bfloat16)
    twiddle_grad = lax.psum(jnp.stack(partials), "seq")
    d_value = lax.dot_general(
        square_mix, grad_now, (((0,), (0,)), ((), ())), preferred_element_type=jnp.float32
    ).astype(jnp.bfloat16)
    grad_square = lax.dot_general(
        grad_now, value, (((1,), (1,)), ((), ())), preferred_element_type=jnp.float32
    )
    d_projected = jnp.concatenate([d_value, d_gate], axis=1)
    win_term = lax.dot_general(
        inputs, d_projected, (((0,), (0,)), ((), ())), preferred_element_type=jnp.float32
    )
    win_share, wout_share = (
        lax.psum_scatter(win_term, "seq", scatter_dimension=0, tiled=True),
        lax.psum_scatter(wout_term, "seq", scatter_dimension=0, tiled=True),
    )
    input_grad = lax.dot_general(
        d_projected, w_in, (((1,), (1,)), ((), ())), preferred_element_type=jnp.float32
    ).astype(jnp.bfloat16)
    handed = from_behind(input_grad, "pipe", -1)
    return (
        mixed_out[None],
        handed[None],
        win_share[None],
        wout_share[None],
        grad_square[None],
        twiddle_grad[None],
    )


def solution(mesh):
    in_specs = (
        P("pipe", "seq", None),
        P("pipe", "seq", None),
        P("pipe", None, None),
        P("pipe", None, None),
        P("pipe", "seq", None),
        P("pipe", None, None, None, None),
    )
    out_specs = (
        P("pipe", "seq", None),
        P("pipe", "seq", None),
        P("pipe", "seq", None),
        P("pipe", "seq", None),
        P("pipe", "seq", None),
        P("pipe", None, None, None, None),
    )
    return jax.shard_map(
        on_device, mesh=mesh, in_specs=in_specs, out_specs=out_specs, check_vma=False
    )
```

profile of v0, /device:TPU:1, one launch (start us, length us, event | category | flops | bytes accessed | tf_op | source)
XLA Modules:
  0.0 686.3 jit_solution(15321098489667302605)
XLA Ops:
  7.2 3.7 fusion.4
  12.3 3.3 collective-permute-start
  15.6 1.5 collective-permute-done
  17.4 13.1 %collective-permute-done.1 = bf16[256,1024]{1,0:T(8,128)(2,1)S(1)} collective-permute-done((bf16[256,1024]{1,0:T(8,128)(2,1)S(1)}, bf16[256,1024]{1,0:T(8,128)(2,1)S(1)}, u32[]{:S(2)}, u32[]{:S(2)}) %collective-permute-start.1) | collective-permute-done | bytes 524320 | tf_op jit(solution)/shard_map/ppermute | solution.py:14
  30.7 1.7 collective-permute-start.2
  32.5 24.0 %collective-permute-done.2 = bf16[256,1024]{1,0:T(8,128)(2,1)S(1)} collective-permute-done((bf16[256,1024]{1,0:T(8,128)(2,1)S(1)}, bf16[256,1024]{1,0:T(8,128)(2,1)S(1)}, u32[]{:S(2)}, u32[]{:S(2)}) %collective-permute-start.2) | collective-permute-done | bytes 524320 | tf_op jit(solution)/shard_map/ppermute | solution.py:14
  56.7 5.1 collective-permute-start.3
  61.8 22.9 %collective-permute-done.3 = bf16[256,1024]{1,0:T(8,128)(2,1)S(1)} collective-permute-done((bf16[256,1024]{1,0:T(8,128)(2,1)S(1)}, bf16[256,1024]{1,0:T(8,128)(2,1)S(1)}, u32[]{:S(2)}, u32[]{:S(2)}) %collective-permute-start.3) | collective-permute-done | bytes 524320 | tf_op jit(solution)/shard_map/ppermute | solution.py:14
  86.1 10.7 %collective-permute-done.4 = bf16[256,1024]{1,0:T(8,128)(2,1)S(1)} collective-permute-done((bf16[256,1024]{1,0:T(8,128)(2,1)S(1)}, bf16[256,1024]{1,0:T(8,128)(2,1)S(1)}, u32[]{:S(2)}, u32[]{:S(2)}) %collective-permute-start.4) | collective-permute-done | bytes 524320 | tf_op jit(solution)/shard_map/ppermute | solution.py:14
  97.1 2.9 collective-permute-start.5
  100.7 8.9 %collective-permute-done.5 = bf16[256,1024]{1,0:T(8,128)(2,1)S(1)} collective-permute-done((bf16[256,1024]{1,0:T(8,128)(2,1)S(1)}, bf16[256,1024]{1,0:T(8,128)(2,1)S(1)}, u32[]{:S(2)}, u32[]{:S(2)}) %collective-permute-start.5) | collective-permute-done | bytes 524320 | tf_op jit(solution)/shard_map/ppermute | solution.py:14
  111.0 2.9 collective-permute-start.6
  113.9 8.7 %collective-permute-done.6 = bf16[256,1024]{1,0:T(8,128)(2,1)S(1)} collective-permute-done((bf16[256,1024]{1,0:T(8,128)(2,1)S(1)}, bf16[256,1024]{1,0:T(8,128)(2,1)S(1)}, u32[]{:S(2)}, u32[]{:S(2)}) %collective-permute-start.6) | collective-permute-done | bytes 524320 | tf_op jit(solution)/shard_map/ppermute | solution.py:14
  123.0 1.5 collective-permute-start.7
  124.5 9.7 %collective-permute-done.7 = bf16[256,1024]{1,0:T(8,128)(2,1)S(1)} collective-permute-done((bf16[256,1024]{1,0:T(8,128)(2,1)S(1)}, bf16[256,1024]{1,0:T(8,128)(2,1)S(1)}, u32[]{:S(2)}, u32[]{:S(2)}) %collective-permute-start.7) | collective-permute-done | bytes 524320 | tf_op jit(solution)/shard_map/ppermute | solution.py:14
  134.6 1.5 collective-permute-start.8
  136.2 23.7 %collective-permute-done.8 = bf16[256,1024]{1,0:T(8,128)(2,1)S(1)} collective-permute-done((bf16[256,1024]{1,0:T(8,128)(2,1)S(1)}, bf16[256,1024]{1,0:T(8,128)(2,1)S(1)}, u32[]{:S(2)}, u32[]{:S(2)}) %collective-permute-start.8) | collective-permute-done | bytes 524320 | tf_op jit(solution)/shard_map/ppermute | solution.py:14
  160.5 18.1 %collective-permute-done.9 = bf16[256,1024]{1,0:T(8,128)(2,1)S(1)} collective-permute-done((bf16[256,1024]{1,0:T(8,128)(2,1)S(1)}, bf16[256,1024]{1,0:T(8,128)(2,1)S(1)}, u32[]{:S(2)}, u32[]{:S(2)}) %collective-permute-start.9) | collective-permute-done | bytes 524320 | tf_op jit(solution)/shard_map/ppermute | solution.py:14
  179.4 13.0 %collective-permute-done.10 = bf16[256,1024]{1,0:T(8,128)(2,1)S(1)} collective-permute-done((bf16[256,1024]{1,0:T(8,128)(2,1)S(1)}, bf16[256,1024]{1,0:T(8,128)(2,1)S(1)}, u32[]{:S(2)}, u32[]{:S(2)}) %collective-permute-start.10) | collective-permute-done | bytes 524320 | tf_op jit(solution)/shard_map/ppermute | solution.py:14
  192.8 1.4 collective-permute-start.11
  194.2 1.5 collective-permute-done.11
  196.2 4.5 convolution_bitcast_fusion
  200.7 9.2 %copy.17 = f32[1024,2048]{1,0:T(8,128)} copy(f32[1024,2048]{0,1:T(8,128)} %convolution_bitcast_fusion) | data formatting | bytes 16777216
  211.2 3.9 fusion.64
  215.1 3.8 fusion.17
  220.4 1.5 fusion.20
  223.0 11.2 %collective-permute-done.12 = bf16[256,1024]{1,0:T(8,128)(2,1)} collective-permute-done((bf16[256,1024]{1,0:T(8,128)(2,1)S(1)}, bf16[256,1024]{1,0:T(8,128)(2,1)}, u32[]{:S(2)}, u32[]{:S(2)}) %collective-permute-start.12) | collective-permute-done | bytes 524320 | tf_op jit(solution)/shard_map/ppermute | solution.py:20
  234.2 121.7 %reduce-scatter.7.cloned.1.call-done = f32[16,2048]{1,0:T(8,128)} async-done(((f32[1024,2048]{1,0:T(8,128)}), f32[16,2048]{1,0:T(8,128)}) %reduce-scatter.7.cloned.1.call-update) | async-done | bytes 131088
  358.1 176.8 %all-reduce.14.cloned.1.call-done = f32[1,6,2,2,1024]{4,3,2,1,0:T(2,128)} async-done(((f32[1,6,2,2,1024]{4,3,2,1,0:T(2,128)}), f32[1,6,2,2,1024]{4,3,2,1,0:T(2,128)}) %all-reduce.14.cloned.1.call-update) | async-done | bytes 98320 | tf_op jit(solution)/shard_map/psum | solution.py:85
  535.0 141.4 %reduce-scatter.5.cloned.1.call-done = f32[16,1024]{1,0:T(8,128)} async-done(((f32[1024,1024]{1,0:T(8,128)}), f32[16,1024]{1,0:T(8,128)}) %reduce-scatter.5.cloned.1.call-update) | async-done | bytes 65552 | tf_op jit(solution)/shard_map/reduce_scatter | solution.py:98
  676.3 1.9 copy.26
  678.2 1.5 copy.27
  (83 shorter events, 14.7 us)
Async XLA Ops:
  7.2 92.8 %copy-start = (bf16[1,1024,1024]{2,1,0:T(8,128)(2,1)S(1)}, bf16[1,1024,1024]{2,1,0:T(8,128)(2,1)}, u32[]{:S(2)}) copy-start(bf16[1,1024,1024]{2,1,0:T(8,128)(2,1)} %param.9) | copy-start | bytes 6291460
  7.2 4.8 copy-start.13
  7.2 8.4 %copy-start.11 = (f32[1,6,2,2,1024]{4,3,2,1,0:T(2,128)S(1)}, f32[1,6,2,2,1024]{4,3,2,1,0:T(2,128)}, u32[]{:S(2)}) copy-start(f32[1,6,2,2,1024]{4,3,2,1,0:T(2,128)} %param.11) | copy-start | bytes 294916
  7.2 348.7 %reduce-scatter.7.cloned.1.call-start = ((), (), s32[]{:S(2)}) async-start(), calls=%async_computation.4 | async-start | bytes 8519680
  11.0 1.0 copy-start.1
  12.3 4.8 collective-permute-start
  17.3 13.2 %collective-permute-start.1 = (bf16[256,1024]{1,0:T(8,128)(2,1)S(1)}, bf16[256,1024]{1,0:T(8,128)(2,1)S(1)}, u32[]{:S(2)}, u32[]{:S(2)}) collective-permute-start(bf16[256,1024]{1,0:T(8,128)(2,1)S(1)} %fusion.26), channel_id=1, source_target_pairs={{0,2},{2,0},{1,3},{3,1},{4,6},{6,4},{5,7},{7,5},{8,10},{10,8},{9,1... | collective-permute-start | bytes 1572872 | tf_op jit(solution)/shard_map/ppermute | solution.py:14
  30.7 25.8 %collective-permute-start.2 = (bf16[256,1024]{1,0:T(8,128)(2,1)S(1)}, bf16[256,1024]{1,0:T(8,128)(2,1)S(1)}, u32[]{:S(2)}, u32[]{:S(2)}) collective-permute-start(bf16[256,1024]{1,0:T(8,128)(2,1)S(1)} %fusion.28), channel_id=1, source_target_pairs={{0,4},{4,0},{1,5},{5,1},{2,6},{6,2},{3,7},{7,3},{8,12},{12,8},{9,1... | collective-permute-start | bytes 1572872 | tf_op jit(solution)/shard_map/ppermute | solution.py:14
  56.5 43.5 %copy-start.10 = (bf16[1,256,1024]{2,1,0:T(8,128)(2,1)S(1)}, bf16[1,256,1024]{2,1,0:T(8,128)(2,1)}, u32[]{:S(2)}) copy-start(bf16[1,256,1024]{2,1,0:T(8,128)(2,1)} %param.7) | copy-start | bytes 1572868
  56.7 28.0 %collective-permute-start.3 = (bf16[256,1024]{1,0:T(8,128)(2,1)S(1)}, bf16[256,1024]{1,0:T(8,128)(2,1)S(1)}, u32[]{:S(2)}, u32[]{:S(2)}) collective-permute-start(bf16[256,1024]{1,0:T(8,128)(2,1)S(1)} %fusion.30), channel_id=1, source_target_pairs={{0,8},{8,0},{1,9},{9,1},{2,10},{10,2},{3,11},{11,3},{4,12},{12,4},... | collective-permute-start | bytes 1572872 | tf_op jit(solution)/shard_map/ppermute | solution.py:14
  85.0 11.9 %collective-permute-start.4 = (bf16[256,1024]{1,0:T(8,128)(2,1)S(1)}, bf16[256,1024]{1,0:T(8,128)(2,1)S(1)}, u32[]{:S(2)}, u32[]{:S(2)}) collective-permute-start(bf16[256,1024]{1,0:T(8,128)(2,1)S(1)} %fusion.32), channel_id=1, source_target_pairs={{0,16},{16,0},{1,17},{17,1},{2,18},{18,2},{3,19},{19,3},{4,20},{20... | collective-permute-start | bytes 1572872 | tf_op jit(solution)/shard_map/ppermute | solution.py:14
  97.1 12.5 %copy-start.2 = (bf16[256,2048]{1,0:T(8,128)(2,1)S(1)}, bf16[256,2048]{1,0:T(8,128)(2,1)}, u32[]{:S(2)}) copy-start(bf16[256,2048]{1,0:T(8,128)(2,1)} %copy-done.1) | copy-start | bytes 3145732
  97.1 12.5 %collective-permute-start.5 = (bf16[256,1024]{1,0:T(8,128)(2,1)S(1)}, bf16[256,1024]{1,0:T(8,128)(2,1)S(1)}, u32[]{:S(2)}, u32[]{:S(2)}) collective-permute-start(bf16[256,1024]{1,0:T(8,128)(2,1)S(1)} %fusion.34), channel_id=1, source_target_pairs={{0,32},{32,0},{1,33},{33,1},{2,34},{34,2},{3,35},{35,3},{4,36},{36... | collective-permute-start | bytes 1572872 | tf_op jit(solution)/shard_map/ppermute | solution.py:14
  111.0 85.2 %copy-start.4 = (bf16[256,1024]{1,0:T(8,128)(2,1)}, bf16[256,1024]{1,0:T(8,128)(2,1)S(1)}, u32[]{:S(2)}) copy-start(bf16[256,1024]{1,0:T(8,128)(2,1)S(1)} %get-tuple-element.38) | copy-start | bytes 1572868
  111.0 11.6 %collective-permute-start.6 = (bf16[256,1024]{1,0:T(8,128)(2,1)S(1)}, bf16[256,1024]{1,0:T(8,128)(2,1)S(1)}, u32[]{:S(2)}, u32[]{:S(2)}) collective-permute-start(bf16[256,1024]{1,0:T(8,128)(2,1)S(1)} %get-tuple-element.30), channel_id=1, source_target_pairs={{0,32},{32,0},{1,33},{33,1},{2,34},{34,2},{3,35},{35,3},{4,36},{36... | collective-permute-start | bytes 1572872 | tf_op jit(solution)/shard_map/ppermute | solution.py:14
  123.0 11.2 %collective-permute-start.7 = (bf16[256,1024]{1,0:T(8,128)(2,1)S(1)}, bf16[256,1024]{1,0:T(8,128)(2,1)S(1)}, u32[]{:S(2)}, u32[]{:S(2)}) collective-permute-start(bf16[256,1024]{1,0:T(8,128)(2,1)S(1)} %get-tuple-element.31), channel_id=1, source_target_pairs={{0,16},{16,0},{1,17},{17,1},{2,18},{18,2},{3,19},{19,3},{4,20},{20... | collective-permute-start | bytes 1572872 | tf_op jit(solution)/shard_map/ppermute | solution.py:14
  134.6 25.3 %collective-permute-start.8 = (bf16[256,1024]{1,0:T(8,128)(2,1)S(1)}, bf16[256,1024]{1,0:T(8,128)(2,1)S(1)}, u32[]{:S(2)}, u32[]{:S(2)}) collective-permute-start(bf16[256,1024]{1,0:T(8,128)(2,1)S(1)} %get-tuple-element.32), channel_id=1, source_target_pairs={{0,8},{8,0},{1,9},{9,1},{2,10},{10,2},{3,11},{11,3},{4,12},{12,4},... | collective-permute-start | bytes 1572872 | tf_op jit(solution)/shard_map/ppermute | solution.py:14
  160.4 18.2 %collective-permute-start.9 = (bf16[256,1024]{1,0:T(8,128)(2,1)S(1)}, bf16[256,1024]{1,0:T(8,128)(2,1)S(1)}, u32[]{:S(2)}, u32[]{:S(2)}) collective-permute-start(bf16[256,1024]{1,0:T(8,128)(2,1)S(1)} %get-tuple-element.33), channel_id=1, source_target_pairs={{0,4},{4,0},{1,5},{5,1},{2,6},{6,2},{3,7},{7,3},{8,12},{12,8},{9,1... | collective-permute-start | bytes 1572872 | tf_op jit(solution)/shard_map/ppermute | solution.py:14
  179.1 13.3 %collective-permute-start.10 = (bf16[256,1024]{1,0:T(8,128)(2,1)S(1)}, bf16[256,1024]{1,0:T(8,128)(2,1)S(1)}, u32[]{:S(2)}, u32[]{:S(2)}) collective-permute-start(bf16[256,1024]{1,0:T(8,128)(2,1)S(1)} %get-tuple-element.34), channel_id=1, source_target_pairs={{0,2},{2,0},{1,3},{3,1},{4,6},{6,4},{5,7},{7,5},{8,10},{10,8},{9,1... | collective-permute-start | bytes 1572872 | tf_op jit(solution)/shard_map/ppermute | solution.py:14
  192.3 3.9 copy-start.6
  192.8 3.0 copy-start.7
  192.8 3.0 collective-permute-start.11
  195.8 5.0 copy-start.14
  196.2 4.5 copy-start.9
  209.9 1.2 copy-start.3
  210.0 325.0 %all-reduce.14.cloned.1.call-start = ((), (), s32[]{:S(2)}) async-start(), calls=%async_computation.3 | async-start | bytes 196608 | tf_op jit(solution)/shard_map/psum | solution.py:85
  210.3 0.6 copy-start.12
  210.9 465.4 %reduce-scatter.5.cloned.1.call-start = ((), (), s32[]{:S(2)}) async-start(), calls=%async_computation.2 | async-start | bytes 4259840 | tf_op jit(solution)/shard_map/reduce_scatter | solution.py:98
  215.1 5.3 copy-start.5
  219.0 3.0 copy-start.8
  219.0 3.0 copy-start.15
  219.0 15.2 %collective-permute-start.12 = (bf16[256,1024]{1,0:T(8,128)(2,1)S(1)}, bf16[256,1024]{1,0:T(8,128)(2,1)}, u32[]{:S(2)}, u32[]{:S(2)}) collective-permute-start(bf16[256,1024]{1,0:T(8,128)(2,1)S(1)} %fusion.17), channel_id=1, source_target_pairs={{64,0},{128,64},{192,128},{65,1},{129,65},{193,129},{66,2},{130,66... | collective-permute-start | bytes 1572872 | tf_op jit(solution)/shard_map/ppermute | solution.py:20
Sparse Core Ops, SparseCore 0:
  210.1 145.7 reduce-scatter.6
  359.9 174.9 all-reduce.13
  539.7 136.6 reduce-scatter.4
where the time goes:
time: 691 us; the launch traced here: 686 us
  waiting for transfers between devices  607 us (88%)
  starting transfers between devices  23.5 us (3%)
  matrix products  20.1 us (3%)
  local copies, waits for them, and re-layouts  16.7 us (2%)
  between operations  14.1 us (2%)
    psum x1, waiting for transfers between devices, on_device(): twiddle_grad = lax.psum(jnp.stack(partials), 'seq')  177 us
    ppermute x12, waiting for transfers between devices, swapped(): return lax.ppermute(block, axis, route)  156 us
    reduce_scatter x1, waiting for transfers between devices, on_device(): lax.psum_scatter(wout_term, 'seq', scatter_dimension=0, tiled=True)  141 us
    unnamed x4, waiting for transfers between devices  122 us
    ppermute x12, starting transfers between devices, swapped(): return lax.ppermute(block, axis, route)  21.9 us
    unnamed x37, local copies, waits for them, and re-layouts  16.7 us
  transfers between devices with their start and end apart: 16, of which 16 were waited for; matrix products, arithmetic and copies ran while one was open for 2% of the time, Pallas kernels for 0%

commit v1 on v0

v1 whole, which is shorter than its diff:
```python
import functools

import jax
import jax.numpy as jnp
from jax import lax
from jax.experimental import pallas as pl
from jax.experimental.pallas import tpu as pltpu
from jax.sharding import PartitionSpec as P

F32 = jnp.float32
BF16 = jnp.bfloat16
MESH = pl.DeviceIdType.MESH
HALVES = 2
LANES = 128


def ring_sizes(count):
    bits = count.bit_length() - 2
    y_bits = bits // 2
    return 1 << y_bits, 1 << (bits - y_bits)


def butterfly(parts, coefs):
    stages = [parts]
    for bit, coef in enumerate(coefs):
        now = stages[-1]
        after = [None] * len(now)
        for low in range(len(now)):
            high = low | 1 << bit
            if high != low:
                after[low] = coef[0] * now[low] + coef[1] * now[high]
                after[high] = coef[2] * now[high] + coef[3] * now[low]
        stages.append(after)
    return stages


def butterfly_back(grads, coefs):
    stages = [grads]
    for bit in range(len(coefs) - 1, -1, -1):
        coef = coefs[bit]
        now = stages[0]
        before = [None] * len(now)
        for low in range(len(now)):
            high = low | 1 << bit
            if high != low:
                before[low] = coef[0] * now[low] + coef[3] * now[high]
                before[high] = coef[2] * now[high] + coef[1] * now[low]
        stages.insert(0, before)
    return stages


def coef_grads(stages, grad_stages, bits):
    totals = []
    for bit in range(bits):
        vals, grads = stages[bit], grad_stages[bit + 1]
        sums = [None] * 4
        for low in range(len(vals)):
            high = low | 1 << bit
            if high != low:
                terms = (
                    grads[low] * vals[low],
                    grads[low] * vals[high],
                    grads[high] * vals[high],
                    grads[high] * vals[low],
                )
                sums = [t if s is None else s + t for s, t in zip(sums, terms)]
        totals += [jnp.sum(s, axis=0, keepdims=True) for s in sums]
    return totals


class Links:
    def __init__(self, ny, nz, send, recv):
        self.ny, self.nz = ny, nz
        self.send, self.recv = send, recv
        self.used = 0
        self.copies = []
        me = lax.axis_index("seq")
        self.c = lax.rem(me, 2)
        self.z = lax.rem(me // 2, nz)
        self.y = me // (2 * nz)

    def seq(self, y, z, c):
        return (y * self.nz + z) * 2 + c

    def z_peer(self, apart):
        return lax.rem(self.z + apart + self.nz, self.nz)

    def y_peer(self, apart):
        return lax.rem(self.y + apart + self.ny, self.ny)

    def put(self, source, target, y, z, c):
        copy = pltpu.make_async_remote_copy(
            src_ref=source,
            dst_ref=target,
            send_sem=self.send.at[self.used],
            recv_sem=self.recv.at[self.used],
            device_id={"seq": self.seq(y, z, c)},
            device_id_type=MESH,
        )
        copy.start()
        self.used += 1
        self.copies.append(copy)
        return copy

    def greet(self):
        barrier = pltpu.get_barrier_semaphore()
        count = 0
        for apart in range(1, self.nz):
            pl.semaphore_signal(
                barrier, inc=1, device_id={"seq": self.seq(self.y, self.z_peer(apart), self.c)}, device_id_type=MESH
            )
            count += 1
        for apart in range(1, self.ny):
            pl.semaphore_signal(
                barrier, inc=1, device_id={"seq": self.seq(self.y_peer(apart), self.z, self.c)}, device_id_type=MESH
            )
            count += 1
        pl.semaphore_signal(
            barrier, inc=1, device_id={"seq": self.seq(self.y, self.z, 1 - self.c)}, device_id_type=MESH
        )
        return barrier, count + 1


def arrived(copies):
    for copy in copies:
        copy.wait_recv()


def mixer_copies(ny, nz):
    return 4 * HALVES * (nz - 1) + 4 * HALVES * (ny - 1) + 2 * HALVES


def mixer_kernel(
    ny, nz, seg0, dseg6, tw, monarch, dseg0, gtw,
    fzin, fzout, fy0, fyin, fyout, fc0, fcin, bcin, by0, byin, byout, bz0, bzin, bzout, send, recv,
):
    links = Links(ny, nz, send, recv)
    y, z, c = links.y, links.z, links.c
    per_y = nz // ny
    z_bits, y_bits = nz.bit_length() - 1, ny.bit_length() - 1
    tiles = seg0.shape[-1] // LANES
    barrier, greeted = links.greet()
    pl.semaphore_wait(barrier, greeted)

    def lanes_of(tile):
        return pl.ds(pl.multiple_of(tile * LANES, LANES), LANES)

    def coefs_of(first_bit, bits, lanes):
        return [[tw[pl.ds((first_bit + b) * 4 + k, 1), lanes] for k in range(4)] for b in range(bits)]

    def z_out(source, target, h):
        target[h, z] = source[h, z]
        return [
            links.put(source.at[h, links.z_peer(p)], target.at[h, z], y, links.z_peer(p), c) for p in range(1, nz)
        ]

    def z_back(source, target, h):
        target[h, z] = source[h, z]
        return [
            links.put(source.at[h, links.z_peer(p)], target.at[h, z], y, links.z_peer(p), c) for p in range(1, nz)
        ]

    def rows_y(which):
        return pl.ds(which * per_y, per_y)

    def y_out(source, target, h):
        target[h, y] = source[h, rows_y(y)]
        return [
            links.put(source.at[h, rows_y(links.y_peer(p))], target.at[h, y], links.y_peer(p), z, c)
            for p in range(1, ny)
        ]

    def y_back(source, target, h):
        target[h, rows_y(y)] = source[h, y]
        return [
            links.put(source.at[h, links.y_peer(p)], target.at[h, rows_y(y)], links.y_peer(p), z, c)
            for p in range(1, ny)
        ]

    def f_z(h):
        @pl.loop(0, tiles)
        def _(tile):
            lanes = lanes_of(tile)
            coefs = coefs_of(1, z_bits, lanes)
            out = butterfly([fzin[h, k, :, lanes].astype(F32) for k in range(nz)], coefs)[-1]
            for k in range(nz):
                fzout[h, k, :, lanes] = out[k].astype(BF16)

    def b_y(h):
        @pl.loop(0, tiles)
        def _(tile):
            lanes = lanes_of(tile)
            coefs = coefs_of(1 + z_bits, y_bits, lanes)
            for r in range(per_y):
                out = butterfly_back([byin[h, k, r, :, lanes].astype(F32) for k in range(ny)], coefs)[0]
                for k in range(ny):
                    byout[h, k, r, :, lanes] = out[k].astype(BF16)

    def add_grads(tile, first_bit, totals):
        for k, total in enumerate(totals):
            row = pl.ds(first_bit * 4 + k, 1)
            gtw[tile, row, :] = gtw[tile, row, :] + total

    def f_y(h):
        @pl.loop(0, tiles)
        def _(tile):
            lanes = lanes_of(tile)
            coefs = coefs_of(1 + z_bits, y_bits, lanes)
            for r in range(per_y):
                stages = butterfly([fyin[h, k, r, :, lanes].astype(F32) for k in range(ny)], coefs)
                grads = butterfly_back([byin[h, k, r, :, lanes].astype(F32) for k in range(ny)], coefs)
                for k in range(ny):
                    fyout[h, k, r, :, lanes] = stages[-1][k].astype(BF16)
                add_grads(tile, 1 + z_bits, coef_grads(stages, grads, y_bits))

    def b_z(h):
        @pl.loop(0, tiles)
        def _(tile):
            lanes = lanes_of(tile)
            coefs = coefs_of(1, z_bits, lanes)
            stages = butterfly([fzin[h, k, :, lanes].astype(F32) for k in range(nz)], coefs)
            grads = butterfly_back([bzin[h, k, :, lanes].astype(F32) for k in range(nz)], coefs)
            for k in range(nz):
                bzout[h, k, :, lanes] = grads[0][k].astype(BF16)
            add_grads(tile, 1, coef_grads(stages, grads, z_bits))

    def b_core(h):
        @pl.loop(0, tiles)
        def _(tile):
            lanes = lanes_of(tile)
            own = jnp.where(c == 0, tw[pl.ds(0, 1), lanes], tw[pl.ds(2, 1), lanes])
            peer = jnp.where(c == 0, tw[pl.ds(3, 1), lanes], tw[pl.ds(1, 1), lanes])
            for k in range(nz):
                by0[h, k, :, lanes] = (
                    own * dseg6[h, k, :, lanes].astype(F32) + peer * bcin[h, k, :, lanes].astype(F32)
                ).astype(BF16)

    def f_core(h):
        @pl.loop(0, tiles)
        def _(tile):
            lanes = lanes_of(tile)
            own = jnp.where(c == 0, tw[pl.ds(0, 1), lanes], tw[pl.ds(2, 1), lanes])
            peer = jnp.where(c == 0, tw[pl.ds(1, 1), lanes], tw[pl.ds(3, 1), lanes])
            sums = [None, None]
            for k in range(nz):
                mine = fc0[h, k, :, lanes].astype(F32)
                other = fcin[h, k, :, lanes].astype(F32)
                grad = dseg6[h, k, :, lanes].astype(F32)
                monarch[h, k, :, lanes] = (own * mine + peer * other).astype(BF16)
                terms = (grad * mine, grad * other)
                sums = [t if s is None else s + t for s, t in zip(sums, terms)]
            for k in range(4):
                total = jnp.sum(sums[k % 2], axis=0, keepdims=True)
                row = pl.ds(k, 1)
                gtw[tile, row, :] = gtw[tile, row, :] + jnp.where(c == k // 2, total, 0.0)

    both = range(HALVES)
    fz = [z_out(seg0, fzin, h) for h in both]
    bc = [links.put(dseg6.at[h], bcin.at[h], y, z, 1 - c) for h in both]
    gtw[...] = jnp.zeros_like(gtw)
    by = []
    for h in both:
        bc[h].wait_recv()
        b_core(h)
        by.append(y_out(by0, byin, h))
    fzb, byb = [], []
    for h in both:
        arrived(fz[h])
        f_z(h)
        fzb.append(z_back(fzout, fy0, h))
        arrived(by[h])
        b_y(h)
        byb.append(y_back(byout, bz0, h))
    bz = []
    for h in both:
        arrived(byb[h])
        bz.append(z_out(bz0, bzin, h))
    fy = []
    for h in both:
        arrived(fzb[h])
        fy.append(y_out(fy0, fyin, h))
    fyb = []
    for h in both:
        arrived(fy[h])
        f_y(h)
        fyb.append(y_back(fyout, fc0, h))
    fc, bzb = [], []
    for h in both:
        arrived(fyb[h])
        fc.append(links.put(fc0.at[h], fcin.at[h], y, z, 1 - c))
        if h == 0:
            arrived(bz[h])
            b_z(h)
            bzb.append(z_back(bzout, dseg0, h))
    for h in both:
        fc[h].wait_recv()
        f_core(h)
    for h in both:
        if h > 0:
            arrived(bz[h])
            b_z(h)
            bzb.append(z_back(bzout, dseg0, h))
    for h in both:
        arrived(bzb[h])
    for copy in links.copies:
        copy.wait_send()


def mixer(ny, nz, seg0, dseg6, tw):
    rows, width = seg0.shape
    inner = rows // (HALVES * nz)
    per_y = nz // ny
    tiles = width // LANES
    shape_z = (HALVES, nz, inner, width)
    shape_y = (HALVES, ny, per_y, inner, width)
    count = mixer_copies(ny, nz)
    vmem = pl.BlockSpec(memory_space=pltpu.VMEM)
    kinds = [
        shape_z, shape_z, shape_z, shape_y, shape_y, shape_z, shape_z,
        shape_z, shape_z, shape_y, shape_y, shape_z, shape_z, shape_z,
    ]
    monarch, dseg0, gtw = pl.pallas_call(
        functools.partial(mixer_kernel, ny, nz),
        out_shape=(
            jax.ShapeDtypeStruct(shape_z, BF16),
            jax.ShapeDtypeStruct(shape_z, BF16),
            jax.ShapeDtypeStruct((tiles, tw.shape[0], LANES), F32),
        ),
        in_specs=[vmem] * 3,
        out_specs=(vmem,) * 3,
        scratch_shapes=[pltpu.VMEM(shape, BF16) for shape in kinds]
        + [pltpu.SemaphoreType.DMA((count,)), pltpu.SemaphoreType.DMA((count,))],
        compiler_params=pltpu.CompilerParams(collective_id=0, has_side_effects=True),
        name="mixer",
    )(seg0.reshape(shape_z), dseg6.reshape(shape_z), tw)
    return monarch.reshape(rows, width), dseg0.reshape(rows, width), gtw


class Chain:
    def __init__(self, size, me, way, steps, own, come, go, ship):
        self.size, self.me, self.way, self.steps = size, me, way, steps
        self.own, self.come, self.go, self.ship = own, come, go, ship
        self.copy = None

    def step(self, at):
        if at >= self.steps:
            return
        dest = lax.rem(self.me + self.way * (self.steps - at) + self.size, self.size)
        source = self.own.at[dest]
        if at > 0:
            self.copy.wait_recv()
            self.go[at - 1] = (self.own[dest].astype(F32) + self.come[at - 1].astype(F32)).astype(BF16)
            source = self.go.at[at - 1]
        self.copy = self.ship(source, self.come.at[at], self.way)

    def last(self):
        if self.steps == 0:
            return None
        self.copy.wait_recv()
        return self.come[self.steps - 1].astype(F32)


def chains_of(size, me, own, come, go, ship):
    longer, shorter = size // 2, size // 2 - 1
    pairs = []
    for part, (ahead, behind) in enumerate(((longer, shorter), (shorter, longer))):
        pairs.append(
            [
                Chain(size, me, 1, ahead, own[part], come[part][0], go[part][0], ship),
                Chain(size, me, -1, behind, own[part], come[part][1], go[part][1], ship),
            ]
        )
    return pairs


def settled(pair, own, me):
    total = own[me].astype(F32)
    for chain in pair:
        value = chain.last()
        if value is not None:
            total = total + value
    return total


def ring_steps(pairs, at):
    for pair in pairs:
        for chain in pair:
            chain.step(at)


def sums_copies(ny, nz):
    return 2 * ((ny - 1) + (nz - 1)) * 2 + 2 * (nz - 1) + (ny - 1) + 2


def sums_kernel(
    ny, nz, c1, cg, cw, gtw, grad_in, win, wout, tw_out, handed,
    z1come, z1go, y1own, y1come, y1go, y2come, y2go, z2own, z2come, z2go,
    tz_in, ty_in, tc_in, tsum, tall, fin, fin_in, send, recv, hand_send, hand_recv,
):
    links = Links(ny, nz, send, recv)
    y, z, c = links.y, links.z, links.c
    pipe = lax.axis_index("pipe")
    pipes = lax.axis_size("pipe")
    barrier, greeted = links.greet()
    for apart in (1, pipes - 1):
        pl.semaphore_signal(
            barrier, inc=1, device_id={"pipe": lax.rem(pipe + apart, pipes)}, device_id_type=MESH
        )
    pl.semaphore_wait(barrier, greeted + 2)

    def hand_copy(target):
        return pltpu.make_async_remote_copy(
            src_ref=grad_in,
            dst_ref=handed,
            send_sem=hand_send,
            recv_sem=hand_recv,
            device_id={"pipe": target},
            device_id_type=MESH,
        )

    @pl.when(pipe > 0)
    def _():
        hand_copy(pipe - 1).start()

    @pl.when(pipe == pipes - 1)
    def _():
        handed[...] = jnp.zeros_like(handed)

    def ship_z(source, target, way):
        return links.put(source, target, y, links.z_peer(way), c)

    def ship_y(source, target, way):
        return links.put(source, target, links.y_peer(way), z, c)

    def halves_of(ref):
        return [[ref.at[part, way] for way in range(2)] for part in range(2)]

    c1_own = [c1.at[0], c1.at[1]]
    first = chains_of(nz, z, c1_own, halves_of(z1come), halves_of(z1go), ship_z)
    c2_own = [cg, cw]
    second = chains_of(ny, y, c2_own, halves_of(y2come), halves_of(y2go), ship_y)
    ring_steps(first, 0)
    ring_steps(second, 0)
    tz = [links.put(gtw.at[links.z_peer(p)], tz_in.at[p - 1], y, links.z_peer(p), c) for p in range(1, nz)]
    z_steps, y_steps = nz // 2, ny // 2
    ring_steps(first, 1)
    arrived(tz)
    total = gtw[z]
    for p in range(nz - 1):
        total = total + tz_in[p]
    tsum[0] = total
    ty = [links.put(tsum.at[0], ty_in.at[p - 1], links.y_peer(p), z, c) for p in range(1, ny)]
    ring_steps(second, 1)
    for at in range(2, z_steps):
        ring_steps(first, at)
    for at in range(2, y_steps):
        ring_steps(second, at)
    arrived(ty)
    total = tsum[0]
    for p in range(ny - 1):
        total = total + ty_in[p]
    tsum[1] = total
    tc = links.put(tsum.at[1], tc_in, y, z, 1 - c)
    for part in range(2):
        y1own[part] = settled(first[part], c1_own[part], z).astype(BF16)
    y1 = chains_of(ny, y, [y1own.at[0], y1own.at[1]], halves_of(y1come), halves_of(y1go), ship_y)
    ring_steps(y1, 0)
    for part in range(2):
        z2own[part] = settled(second[part], c2_own[part], y).astype(BF16)
    z2 = chains_of(nz, z, [z2own.at[0], z2own.at[1]], halves_of(z2come), halves_of(z2go), ship_z)
    ring_steps(z2, 0)
    tc.wait_recv()
    tall[z] = tsum[1] + tc_in[...]
    ta = [links.put(tall.at[z], tall.at[z], y, links.z_peer(p), c) for p in range(1, nz)]
    for at in range(1, y_steps):
        ring_steps(y1, at)
    for at in range(1, z_steps):
        ring_steps(z2, at)
    v_part = y1own.shape[-1]
    o_part = z2own.shape[-1]
    for part in range(2):
        fin[:, part * v_part : (part + 1) * v_part] = settled(y1[part], y1own.at[part], y)
    for part in range(2):
        start = 2 * v_part + part * o_part
        fin[:, start : start + o_part] = settled(z2[part], z2own.at[part], z)
    mine = win.shape[0]
    fc = links.put(fin.at[pl.ds(mine * (1 - c), mine)], fin_in, y, z, 1 - c)
    arrived(ta)
    for k in range(nz):
        tw_out[:, k * LANES : (k + 1) * LANES] = tall[k]
    width = win.shape[1] // 2
    half = width // 2

    def lay(rows_of, core):
        win[:, pl.ds(pl.multiple_of(core * half, half), half)] = rows_of(0, half)
        win[:, pl.ds(pl.multiple_of(width + core * half, half), half)] = rows_of(half, half)
        wout[:, pl.ds(pl.multiple_of(core * half, half), half)] = rows_of(2 * half, half)

    lay(lambda start, size: fin[pl.ds(mine * c, mine), pl.ds(start, size)], c)
    fc.wait_recv()
    lay(lambda start, size: fin_in[:, pl.ds(start, size)], 1 - c)
    for copy in links.copies:
        copy.wait_send()

    @pl.when(pipe < pipes - 1)
    def _():
        hand_copy(pipe).wait_recv()

    @pl.when(pipe > 0)
    def _():
        hand_copy(pipe - 1).wait_send()


def sums(ny, nz, c1, cg, cw, gtw, grad_in):
    block, v_part = c1.shape[-2:]
    o_part = cg.shape[-1]
    width = 4 * v_part
    own_rows = block // 2
    tiles, tw_rows, _ = gtw.shape
    count = sums_copies(ny, nz)
    vmem = pl.BlockSpec(memory_space=pltpu.VMEM)
    z_steps, y_steps = nz // 2, ny // 2
    scratch = [
        pltpu.VMEM((2, 2, z_steps, ny, block, v_part), BF16),
        pltpu.VMEM((2, 2, z_steps, ny, block, v_part), BF16),
        pltpu.VMEM((2, ny, block, v_part), BF16),
        pltpu.VMEM((2, 2, y_steps, block, v_part), BF16),
        pltpu.VMEM((2, 2, y_steps, block, v_part), BF16),
        pltpu.VMEM((2, 2, y_steps, nz, block, o_part), BF16),
        pltpu.VMEM((2, 2, y_steps, nz, block, o_part), BF16),
        pltpu.VMEM((2, nz, block, o_part), BF16),
        pltpu.VMEM((2, 2, z_steps, block, o_part), BF16),
        pltpu.VMEM((2, 2, z_steps, block, o_part), BF16),
        pltpu.VMEM((nz - 1, tw_rows, LANES), F32),
        pltpu.VMEM((ny - 1, tw_rows, LANES), F32),
        pltpu.VMEM((tw_rows, LANES), F32),
        pltpu.VMEM((2, tw_rows, LANES), F32),
        pltpu.VMEM((nz, tw_rows, LANES), F32),
        pltpu.VMEM((block, 2 * v_part + 2 * o_part), F32),
        pltpu.VMEM((own_rows, 2 * v_part + 2 * o_part), F32),
        pltpu.SemaphoreType.DMA((count,)),
        pltpu.SemaphoreType.DMA((count,)),
        pltpu.SemaphoreType.DMA,
        pltpu.SemaphoreType.DMA,
    ]
    return pl.pallas_call(
        functools.partial(sums_kernel, ny, nz),
        out_shape=(
            jax.ShapeDtypeStruct((own_rows, 2 * width), F32),
            jax.ShapeDtypeStruct((own_rows, width), F32),
            jax.ShapeDtypeStruct((tw_rows, tiles * LANES), F32),
            jax.ShapeDtypeStruct(grad_in.shape, BF16),
        ),
        in_specs=[vmem] * 5,
        out_specs=(vmem,) * 4,
        scratch_shapes=scratch,
        compiler_params=pltpu.CompilerParams(collective_id=1, has_side_effects=True),
        name="sums",
    )(c1, cg, cw, gtw, grad_in)


def sibling(value):
    count = lax.axis_size("seq")
    return lax.ppermute(value, "seq", [(k, k ^ 1) for k in range(count)])


def contract_rows(left, right):
    return lax.dot_general(left, right, (((0,), (0,)), ((), ())), preferred_element_type=F32)


def on_device(acts, cotan, proj_in, proj_out, block_mix, twiddle):
    inputs, grad_out = acts[0], cotan[0]
    w_in, w_out, square_mix = proj_in[0], proj_out[0], block_mix[0]
    tw = twiddle[0].reshape(-1, twiddle.shape[-1])
    row_count, width = inputs.shape
    ny, nz = ring_sizes(lax.axis_size("seq"))
    core = lax.rem(lax.axis_index("seq"), 2)
    half = width // 2

    def columns(value, which):
        return lax.dynamic_slice_in_dim(value, which * half, half, 1)

    inputs_2 = jnp.concatenate([inputs, sibling(inputs)], axis=0)
    cotan_2 = jnp.concatenate([columns(grad_out, core), sibling(columns(grad_out, 1 - core))], axis=0)
    projected = jnp.dot(inputs, w_in, preferred_element_type=F32).astype(BF16)
    value, gate = projected[:, :width], projected[:, width:]
    seg0 = jnp.dot(square_mix, value, preferred_element_type=F32).astype(BF16)
    d_hidden = lax.dot_general(
        grad_out, w_out, (((1,), (1,)), ((), ())), preferred_element_type=F32
    ).astype(BF16)
    gate_f = gate.astype(F32)
    dseg6 = (d_hidden.astype(F32) * gate_f).astype(BF16)
    monarch, dseg0, gtw = mixer(ny, nz, seg0, dseg6, tw)
    monarch_f = monarch.astype(F32)
    hidden = (monarch_f * gate_f).astype(BF16)
    d_gate = (d_hidden.astype(F32) * monarch_f).astype(BF16)
    mixed_out = jnp.dot(hidden, w_out, preferred_element_type=F32).astype(BF16)
    d_value = contract_rows(square_mix, dseg0).astype(BF16)
    grad_square = lax.dot_general(
        dseg0, value, (((1,), (1,)), ((), ())), preferred_element_type=F32
    )
    d_projected = jnp.concatenate([d_value, d_gate], axis=1)
    input_grad = lax.dot_general(
        d_projected, w_in, (((1,), (1,)), ((), ())), preferred_element_type=F32
    ).astype(BF16)
    hidden_2 = jnp.concatenate([hidden, sibling(hidden)], axis=0)
    d_gate_2 = jnp.concatenate([columns(d_gate, core), sibling(columns(d_gate, 1 - core))], axis=0)
    d_value_2 = jnp.concatenate([columns(d_value, core), sibling(columns(d_value, 1 - core))], axis=0)
    block = width // (ny * nz)
    cg = contract_rows(inputs_2, d_gate_2).astype(BF16).reshape(ny, nz, block, half)
    cw = contract_rows(hidden_2, cotan_2).astype(BF16).reshape(ny, nz, block, half)
    c1 = contract_rows(inputs_2, d_value_2).astype(BF16).reshape(ny, nz, block, 2, half // 2)
    c1 = jnp.transpose(c1, (3, 1, 0, 2, 4))
    win, wout, tw_grad, handed = sums(ny, nz, c1, cg, cw, gtw, input_grad)
    return (
        mixed_out[None],
        handed[None],
        win[None],
        wout[None],
        grad_square[None],
        tw_grad.reshape(twiddle.shape),
    )


def solution(mesh):
    in_specs = (
        P("pipe", "seq", None),
        P("pipe", "seq", None),
        P("pipe", None, None),
        P("pipe", None, None),
        P("pipe", "seq", None),
        P("pipe", None, None, None, None),
    )
    out_specs = (
        P("pipe", "seq", None),
        P("pipe", "seq", None),
        P("pipe", "seq", None),
        P("pipe", "seq", None),
        P("pipe", "seq", None),
        P("pipe", None, None, None, None),
    )
    return jax.shard_map(
        on_device, mesh=mesh, in_specs=in_specs, out_specs=out_specs, check_vma=False
    )
```

time: 691 us -> 145 us (0.21)
  waiting for transfers between devices: 607 us -> 0.01 us
  Pallas kernels: 0 us -> 102 us
  starting transfers between devices: 23.5 us -> 4.19 us
  between operations: 14.1 us -> 0.76 us
    psum x1 -> x0, waiting for transfers between devices: 177 us -> none  [on_device(): twiddle_grad = lax.psum(jnp.stack(partials), 'seq')]
    ppermute x13 -> x5, waiting for transfers between devices: 167 us -> 0.01 us  [sibling(): return lax.ppermute(value, 'seq', [(k, k ^ 1) for k in range(count)])]
    reduce_scatter x1 -> x0, waiting for transfers between devices: 141 us -> none  [on_device(): lax.psum_scatter(wout_term, 'seq', scatter_dimension=0, tiled=True)]
    unnamed x4 -> x0, waiting for transfers between devices: 122 us -> none
    pallas_call x0 -> x2, Pallas kernels: none -> 102 us  [the longest x1 59.8 us: mixer(): pl.pallas_call(functools.partial(mixer_kernel, ny, nz), out_shape=(jax.Sh...]
    ppermute x13 -> x5, starting transfers between devices: 23.3 us -> 4.19 us  [sibling(): return lax.ppermute(value, 'seq', [(k, k ^ 1) for k in range(count)])]
    unnamed x37 -> x19, local copies, waits for them, and re-layouts: 16.7 us -> 4.95 us
    dot_general x7 -> x8, matrix products: 15.5 us -> 17.3 us  [the longest x4 8.93 us: contract_rows(): lax.dot_general(left, right, (((0,), (0,)), ((), ())), preferred_element_...]
  transfers between devices with their start and end apart: 16 -> 5, of which waited for: 16 -> 0; matrix products, arithmetic and copies ran while one was open for 2% -> 18% of each run, Pallas kernels for 0% -> 41%
where the time goes in v1:
time: 145 us; the launch traced here: 144 us
  Pallas kernels  102 us (70%)
  matrix products  21.1 us (15%)
  local copies, waits for them, and re-layouts  13.5 us (9%)
  starting transfers between devices  4.19 us (3%)
  other arithmetic  2.48 us (2%)
    pallas_call x1, Pallas kernels, mixer(): pl.pallas_call(functools.partial(mixer_kernel, ny, nz), out_shape=(jax.Sh...  59.8 us
    pallas_call x1, Pallas kernels, sums(): pl.pallas_call(functools.partial(sums_kernel, ny, nz), out_shape=(jax.Sha...  42.7 us
    dot_general x4, matrix products, contract_rows(): lax.dot_general(left, right, (((0,), (0,)), ((), ())), preferred_element_...  8.93 us
    unnamed x19, local copies, waits for them, and re-layouts  4.95 us
    ppermute x5, starting transfers between devices, sibling(): return lax.ppermute(value, 'seq', [(k, k ^ 1) for k in range(count)])  4.19 us
    dot_general x1, matrix products, on_device(): projected = jnp.dot(inputs, w_in, preferred_element_type=F32).astype(BF16)  3.66 us
  transfers between devices with their start and end apart: 5, of which 0 were waited for; matrix products, arithmetic and copies ran while one was open for 18% of the time, Pallas kernels for 41%

profile of v1, /device:TPU:1, one launch (start us, length us, event | category | flops | bytes accessed | tf_op | source)
XLA Modules:
  0.0 144.5 jit_solution(8063835313589047356)
XLA Ops:
  0.6 0.0 copy-start
  0.7 1.9 %dynamic-slice_bitcast_fusion.1 = (bf16[256,512]{1,0:T(8,128)(2,1)S(1)}, bf16[256,512]{1,0:T(8,128)(2,1)}) fusion(bf16[1,256,1024]{2,1,0:T(8,128)(2,1)} %param.7, s32[]{:T(128)S(6)} %select_n.4, s32[]{:T(128)S(6)} %select_n.5), kind=kLoop, calls=%fused_computation.46 | loop fusion | bytes 1048584 | tf_op jit(solution)/shard_map/dynamic_slice | solution.py:581
  2.6 3.2 %collective-permute-start.4 = (bf16[256,512]{1,0:T(8,128)(2,1)}, bf16[256,512]{1,0:T(8,128)(2,1)}, u32[]{:S(2)}, u32[]{:S(2)}) collective-permute-start(bf16[256,512]{1,0:T(8,128)(2,1)} %get-tuple-element.21), channel_id=1, source_target_pairs={{0,1},{1,0},{2,3},{3,2},{4,5},{5,4},{6,7},{7,6},{8,9},{9,8},{10,11... | collective-permute-start | bytes 786440 | tf_op jit(solution)/shard_map/ppermute | solution.py:564
  5.8 1.6 %reshape_squeeze.3.tw = f32[24,1024]{1,0:T(8,128)} reshape(f32[1,6,2,2,1024]{4,3,2,1,0:T(2,128)} %param.11) | data formatting | bytes 196608 | tf_op jit(solution)/shard_map/reshape;squeeze | solution.py:574
  7.4 3.7 %fusion.4 = bf16[256,2048]{1,0:T(8,128)(2,1)S(1)} fusion(bf16[1,1024,2048]{2,1,0:T(8,128)(2,1)} %param.8, bf16[1,256,1024]{2,1,0:T(8,128)(2,1)} %param.6), kind=kOutput, calls=%fused_computation.4 | convolution fusion | flops 1074266112 | bytes 5767168 | tf_op jit(solution)/shard_map/dot_general | solution.py:585
  11.1 1.1 convolution_convert_fusion.3
  12.2 1.7 %fusion.23 = (bf16[256,1024]{1,0:T(8,128)(2,1)}, bf16[256,1024]{1,0:T(8,128)(2,1)}) fusion(bf16[256,2048]{1,0:T(8,128)(2,1)S(1)} %fusion.4, bf16[1,1024,1024]{2,1,0:T(8,128)(2,1)S(1)} %copy-done, bf16[1,256,1024]{2,1,0:T(8,128)(2,1)S(1)} %copy-done.2), kind=kOutput, calls=%fused_computation.22 | convolution fusion | flops 538181632 | bytes 4194304 | tf_op jit(solution)/shard_map/dot_general | solution.py:588
  13.9 59.8 %mixer.1 = (bf16[2,8,16,1024]{3,2,1,0:T(8,128)(2,1)}, bf16[2,8,16,1024]{3,2,1,0:T(8,128)(2,1)}, f32[8,24,128]{2,1,0:T(8,128)}) custom-call(bf16[2,8,16,1024]{3,2,1,0:T(8,128)(2,1)} %bitcast.72, bf16[2,8,16,1024]{3,2,1,0:T(8,128)(2,1)} %bitcast.73, f32[24,1024]{1,0:T(8,128)} %reshape_squeeze.3.tw), custom_call_target="tpu_custom_call" | custom-call | tf_op jit(solution)/shard_map/mixer/pallas_call | solution.py:322
  73.7 0.0 copy-start.5
  73.7 2.5 %fusion.25 = (bf16[256,1024]{1,0:T(8,128)(2,1)S(1)}, bf16[256,1024]{1,0:T(8,128)(2,1)}) fusion(bf16[256,1024]{1,0:T(8,128)(2,1)} %get-tuple-element.29, bf16[2,8,16,1024]{3,2,1,0:T(8,128)(2,1)} %get-tuple-element.13, bf16[256,2048]{1,0:T(8,128)(2,1)S(1)} %fusion.4), kind=kLoop, calls=%fused_computation.24 | loop fusion | flops 1835008 | bytes 2621440 | tf_op jit(solution)/shard_map/convert_element_type | solution.py:596
  76.2 0.9 constant_dynamic-slice_fusion.1
  77.0 0.4 collective-permute-start.2
  77.4 0.3 convolution_convert_fusion.4
  77.8 0.2 collective-permute-start.1
  78.0 0.4 collective-permute-start.3
  78.4 2.1 %fusion.17.grad_in = bf16[256,1024]{1,0:T(8,128)(2,1)} fusion(bf16[1,1024,2048]{2,1,0:T(8,128)(2,1)S(1)} %copy-done.5, bf16[256,1024]{1,0:T(8,128)(2,1)S(1)} %get-tuple-element.24, bf16[256,1024]{1,0:T(8,128)(2,1)S(1)} %bitcast.69), kind=kOutput, calls=%fused_computation.19 | convolution fusion | flops 1076101120 | bytes 5767168 | tf_op jit(solution)/shard_map/dot_general | solution.py:603
  80.5 2.6 %fusion.20 = bf16[1,256,1024]{2,1,0:T(8,128)(2,1)} fusion(bf16[256,1024]{1,0:T(8,128)(2,1)} %get-tuple-element.25, bf16[1,1024,1024]{2,1,0:T(8,128)(2,1)S(1)} %copy-done), kind=kOutput, calls=%fused_computation.20 | convolution fusion | flops 537133056 | bytes 3145728 | tf_op jit(solution)/shard_map/dot_general | solution.py:597
  83.1 1.0 convolution_bitcast_fusion
  84.1 0.0 collective-permute-done.1
  84.1 0.0 collective-permute-done
  84.2 2.8 %convolution_convert_fusion.2 = bf16[1024,512]{1,0:T(8,128)(2,1)} fusion(bf16[256,1024]{1,0:T(8,128)(2,1)} %collective-permute-done, bf16[256,1024]{1,0:T(8,128)(2,1)S(1)} %bitcast.80, bf16[256,512]{1,0:T(8,128)(2,1)S(1)} %collective-permute-done.1, bf16[256,512]{1,0:T(8,128)(2,1)S(1)} %get-tuple-element.26), kind=kOutput, calls=%fused_computation.11 | convolution fusion | flops 540540928 | bytes 2621440 | tf_op jit(solution)/shard_map/dot_general | solution.py:568
  86.9 1.3 reshape.41
  88.3 0.0 copy-start.7
  88.3 1.2 copy.17
  89.5 0.0 collective-permute-done.2
  89.5 2.8 %convolution_convert_fusion.1 = bf16[1024,512]{1,0:T(8,128)(2,1)} fusion(bf16[256,1024]{1,0:T(8,128)(2,1)} %collective-permute-done, bf16[256,1024]{1,0:T(8,128)(2,1)S(1)} %bitcast.81, bf16[256,512]{1,0:T(8,128)(2,1)} %collective-permute-done.2, bf16[256,512]{1,0:T(8,128)(2,1)S(1)} %copy-done.4), kind=kOutput, calls=%fused_computation.10 | convolution fusion | flops 540540928 | bytes 2621440 | tf_op jit(solution)/shard_map/dot_general | solution.py:568
  92.3 3.0 %convolution_convert_fusion = bf16[1024,512]{1,0:T(8,128)(2,1)} fusion(bf16[256,1024]{1,0:T(8,128)(2,1)} %collective-permute-done.3, bf16[256,1024]{1,0:T(8,128)(2,1)} %get-tuple-element.25, bf16[256,512]{1,0:T(8,128)(2,1)} %collective-permute-done.4, bf16[256,512]{1,0:T(8,128)(2,1)S(1)} %get-tuple-element.20), kind=kOutput, calls=%fused_computation.9 | convolution fusion | flops 540540928 | bytes 2621440 | tf_op jit(solution)/shard_map/dot_general | solution.py:568
  95.3 42.7 %sums.1 = (f32[16,2048]{1,0:T(8,128)}, f32[16,1024]{1,0:T(8,128)}, f32[24,1024]{1,0:T(8,128)}, bf16[256,1024]{1,0:T(8,128)(2,1)}) custom-call(bf16[2,8,4,32,256]{4,3,2,1,0:T(8,128)(2,1)} %bitcast.68, bf16[4,8,32,512]{3,2,1,0:T(8,128)(2,1)} %bitcast.74, bf16[4,8,32,512]{3,2,1,0:T(8,128)(2,1)} %bitcast.75, f32[8,24,128]{2,1,0:T(8,128)} %get-tuple-element.15.gtw, ...), custom_call_target="tpu_custom_call" | custom-call | tf_op jit(solution)/shard_map/sums/pallas_call | solution.py:546
  138.0 1.6 %reshape.44 = f32[1,6,2,2,1024]{4,3,2,1,0:T(2,128)} reshape(f32[24,1024]{1,0:T(8,128)} %get-tuple-element.19) | data formatting | bytes 196608 | tf_op jit(solution)/shard_map/reshape | solution.py:621
  139.6 1.9 %copy.21 = bf16[1,256,1024]{2,1,0:T(8,128)(2,1)} copy(bf16[1,256,1024]{2,1,0:T(8,128)(2,1)} %bitcast.76) | data formatting | bytes 1048576
  141.4 1.6 %copy.22 = f32[1,16,2048]{2,1,0:T(8,128)} copy(f32[1,16,2048]{2,1,0:T(8,128)} %bitcast.77) | data formatting | bytes 262144
  143.0 1.5 %copy.23 = f32[1,16,1024]{2,1,0:T(8,128)} copy(f32[1,16,1024]{2,1,0:T(8,128)} %bitcast.78) | data formatting | bytes 131072
  (17 shorter events, 0.1 us)
Async XLA Ops:
  0.6 11.6 %copy-start = (bf16[1,1024,1024]{2,1,0:T(8,128)(2,1)S(1)}, bf16[1,1024,1024]{2,1,0:T(8,128)(2,1)}, u32[]{:S(2)}) copy-start(bf16[1,1024,1024]{2,1,0:T(8,128)(2,1)} %param.9) | copy-start | bytes 6291460
  2.6 89.7 %collective-permute-start.4 = (bf16[256,512]{1,0:T(8,128)(2,1)}, bf16[256,512]{1,0:T(8,128)(2,1)}, u32[]{:S(2)}, u32[]{:S(2)}) collective-permute-start(bf16[256,512]{1,0:T(8,128)(2,1)} %get-tuple-element.21), channel_id=1, source_target_pairs={{0,1},{1,0},{2,3},{3,2},{4,5},{5,4},{6,7},{7,6},{8,9},{9,8},{10,11... | collective-permute-start | bytes 786440 | tf_op jit(solution)/shard_map/ppermute | solution.py:564
  5.8 78.3 %collective-permute-start = (bf16[256,1024]{1,0:T(8,128)(2,1)}, bf16[256,1024]{1,0:T(8,128)(2,1)}, u32[]{:S(2)}, u32[]{:S(2)}) collective-permute-start(bf16[256,1024]{1,0:T(8,128)(2,1)} %bitcast.79), channel_id=1, source_target_pairs={{0,1},{1,0},{2,3},{3,2},{4,5},{5,4},{6,7},{7,6},{8,9},{9,8},{10,11... | collective-permute-start | bytes 1572872 | tf_op jit(solution)/shard_map/ppermute | solution.py:564
  7.4 3.7 %copy-start.3 = (bf16[1,256,256]{2,1,0:T(8,128)(2,1)S(1)}, bf16[1,256,256]{2,1,0:T(8,128)(2,1)}, u32[]{:S(2)}) copy-start(bf16[1,256,256]{2,1,0:T(8,128)(2,1)} %param.10) | copy-start | bytes 393220
  7.4 4.8 %copy-start.2 = (bf16[1,256,1024]{2,1,0:T(8,128)(2,1)S(1)}, bf16[1,256,1024]{2,1,0:T(8,128)(2,1)}, u32[]{:S(2)}) copy-start(bf16[1,256,1024]{2,1,0:T(8,128)(2,1)} %param.7) | copy-start | bytes 1572868
  73.7 3.8 %copy-start.1 = (bf16[2,8,16,1024]{3,2,1,0:T(8,128)(2,1)S(1)}, bf16[2,8,16,1024]{3,2,1,0:T(8,128)(2,1)}, u32[]{:S(2)}) copy-start(bf16[2,8,16,1024]{3,2,1,0:T(8,128)(2,1)} %get-tuple-element.14) | copy-start | bytes 1572868
  73.7 4.7 %copy-start.5 = (bf16[1,1024,2048]{2,1,0:T(8,128)(2,1)S(1)}, bf16[1,1024,2048]{2,1,0:T(8,128)(2,1)}, u32[]{:S(2)}) copy-start(bf16[1,1024,2048]{2,1,0:T(8,128)(2,1)} %param.8) | copy-start | bytes 12582916
  77.0 12.5 %collective-permute-start.2 = (bf16[256,512]{1,0:T(8,128)(2,1)}, bf16[256,512]{1,0:T(8,128)(2,1)}, u32[]{:S(2)}, u32[]{:S(2)}) collective-permute-start(bf16[256,512]{1,0:T(8,128)(2,1)} %get-tuple-element.23), channel_id=1, source_target_pairs={{0,1},{1,0},{2,3},{3,2},{4,5},{5,4},{6,7},{7,6},{8,9},{9,8},{10,11... | collective-permute-start | bytes 786440 | tf_op jit(solution)/shard_map/ppermute | solution.py:564
  77.8 6.3 %collective-permute-start.1 = (bf16[256,512]{1,0:T(8,128)(2,1)S(1)}, bf16[256,512]{1,0:T(8,128)(2,1)S(1)}, u32[]{:S(2)}, u32[]{:S(2)}) collective-permute-start(bf16[256,512]{1,0:T(8,128)(2,1)S(1)} %get-tuple-element.27), channel_id=1, source_target_pairs={{0,1},{1,0},{2,3},{3,2},{4,5},{5,4},{6,7},{7,6},{8,9},{9,8},{10,11... | collective-permute-start | bytes 786440 | tf_op jit(solution)/shard_map/ppermute | solution.py:564
  78.0 14.3 %collective-permute-start.3 = (bf16[256,1024]{1,0:T(8,128)(2,1)}, bf16[256,1024]{1,0:T(8,128)(2,1)}, u32[]{:S(2)}, u32[]{:S(2)}) collective-permute-start(bf16[256,1024]{1,0:T(8,128)(2,1)} %get-tuple-element.25), channel_id=1, source_target_pairs={{0,1},{1,0},{2,3},{3,2},{4,5},{5,4},{6,7},{7,6},{8,9},{9,8},{10,11... | collective-permute-start | bytes 1572872 | tf_op jit(solution)/shard_map/ppermute | solution.py:564
  80.5 3.7 %copy-start.6 = (bf16[1,256,1024]{2,1,0:T(8,128)(2,1)S(1)}, bf16[1,256,1024]{2,1,0:T(8,128)(2,1)}, u32[]{:S(2)}) copy-start(bf16[1,256,1024]{2,1,0:T(8,128)(2,1)} %param.6) | copy-start | bytes 1572868
  88.3 1.2 copy-start.4
  88.3 1.2 copy-start.7
